TPU v7x, 32 devices: a whole 2x2x4 slice. The times are simulated.
32 devices in a mesh: row: 8 (over z, y), col: 4 (over x, core).
Axes of the slice: x: 2, y: 2, z: 4, core: 2. Of those that a mesh axis runs over, the one named last changes fastest.
Arguments:
- hidden_in: bfloat16 [16384, 1024], P(('row', 'col')), may hold values from -6 to 6
- teacher: float32 [16384, 1024], P(('row', 'col')), may hold values from -6 to 6
- valid_mask: int32 [16384], replicated, may hold values from 0 to 1, as said below
- first_gain: float32 [1024], replicated, may hold values from 0.1 to 1.9
- second_gain: float32 [1024], replicated, may hold values from 0.1 to 1.9
- attention_in: bfloat16 [3, 1024, 1024], P(None, 'col', 'row'), may hold values from -0.1875 to 0.1875
- attention_out: bfloat16 [1024, 1024], P('row', 'col'), may hold values from -6 to 6
- feed_in: bfloat16 [2, 2624, 1024], P(None, 'col', 'row'), may hold values from -0.1875 to 0.1875
- feed_out: bfloat16 [1024, 2624], P('row', 'col'), may hold values from -0.125 to 0.125
Outputs:
- layer_out: bfloat16 [16384, 1024], P(('row', 'col'))
- loss: float32 [], replicated
- grad_input: float32 [16384, 1024], P(('row', 'col'))
- grad_first_gain: float32 [1024], replicated
- grad_second_gain: float32 [1024], replicated
- grad_attention_in: float32 [3, 1024, 1024], P(None, 'col', 'row')
- grad_attention_out: float32 [1024, 1024], P('row', 'col')
- grad_feed_in: float32 [2, 2624, 1024], P(None, 'col', 'row')
- grad_feed_out: float32 [1024, 2624], P('row', 'col')
Inputs may be any that keep to these rules, and one draw needn't show every extreme that they name: `valid_mask`: 1 marks a token that serves as a key and counts in the loss; the first token of every sequence of 2048 is 1.
All inputs are finite; a program needn't handle non-finite values.
Results may differ from a plain program's by a relative error of at most 0.012.
Values may be sent and summed in bfloat16 or wider, within the bound.
No kernel may reach another device: no remote copies, remote signals or barrier semaphores. Data moves between devices by JAX's collectives and lax.ppermute only.
A program may use at most 256 MiB of HBM per device.

v0:
```python
import jax
import jax.numpy as jnp
from jax import lax
from jax.sharding import PartitionSpec as P

D = 1024
HD = 64
SEQ_LEN = 2048
EPSILON = 1e-05
ROPE_BASE = 160000.0
FLOOR_SCORE = -1e30


def layer_norm(values, gain):
    center = values - jnp.mean(values, axis=1, keepdims=True)
    inverse = lax.rsqrt(jnp.mean(center * center, axis=1, keepdims=True) + EPSILON)
    normed = center * inverse
    return (normed, inverse, (normed * gain).astype(jnp.bfloat16))


def norm_back(grad_low, normed, inverse, gain):
    scaled = grad_low * gain
    inner = jnp.mean(scaled * normed, axis=1, keepdims=True)
    centered = scaled - jnp.mean(scaled, axis=1, keepdims=True)
    return (inverse * (centered - normed * inner), jnp.sum(grad_low * normed, axis=0))


def rotary_tables(rows, width):
    half = width // 2
    frequency = ROPE_BASE ** (-(jnp.arange(half, dtype=jnp.float32) * 2.0) / width)
    place = (jnp.arange(rows, dtype=jnp.int32) % SEQ_LEN).astype(jnp.float32)
    angle = place[:, None] * frequency[None, :]
    angle = jnp.concatenate([angle, angle], axis=1)
    return (jnp.cos(angle), jnp.sin(angle))


def rotate(values, cosine, sine):
    half = values.shape[-1] // 2
    turned = jnp.concatenate([-values[..., half:], values[..., :half]], axis=-1)
    return values * cosine[:, None, :] + turned * sine[:, None, :]


def rotate_back(grads, cosine, sine):
    half = grads.shape[-1] // 2
    moved = grads * sine[:, None, :]
    turned = jnp.concatenate([moved[..., half:], -moved[..., :half]], axis=-1)
    return grads * cosine[:, None, :] + turned


def block_scores(query, keys, live, start, block):
    base = start // SEQ_LEN * SEQ_LEN
    picked = lax.dynamic_slice_in_dim(query, start, block, 0)
    window = lax.dynamic_slice_in_dim(keys, base, SEQ_LEN, 0)
    allowed = lax.dynamic_slice_in_dim(live, base, SEQ_LEN, 0)
    scores = jnp.einsum(
        "qhd,khd->hqk", picked, window, preferred_element_type=jnp.float32
    ) * query.shape[2] ** (-0.5)
    return (jnp.where(allowed[None, None, :] > 0, scores, FLOOR_SCORE), picked, window, base)


def attend(query, keys, values, live):
    rows, heads, width = query.shape
    block = min(512, SEQ_LEN)

    def one_block(index):
        start = index * block
        scores, picked, window, base = block_scores(query, keys, live, start, block)
        seq_values = lax.dynamic_slice_in_dim(values, base, SEQ_LEN, 0)
        top = jnp.max(scores, axis=2, keepdims=True)
        weights = jnp.exp(scores - top)
        total = jnp.sum(weights, axis=2, keepdims=True)
        probs = (weights / total).astype(jnp.bfloat16)
        mixed = jnp.einsum("hqk,khd->qhd", probs, seq_values, preferred_element_type=jnp.float32)
        return (mixed.astype(jnp.bfloat16), (top + jnp.log(total))[:, :, 0])

    mixed, log_total = lax.map(one_block, jnp.arange(rows // block, dtype=jnp.int32))
    return (mixed.reshape(rows, heads * width), log_total)


def attend_back(query, keys, values, live, log_total, grad_mixed):
    rows, heads, width = query.shape
    block = min(512, SEQ_LEN)
    scale = width ** (-0.5)
    zeros = jnp.zeros((rows, heads, width), jnp.float32)

    def one_block(index, carry):
        grad_query, grad_keys, grad_values = carry
        start = index * block
        scores, picked, window, base = block_scores(query, keys, live, start, block)
        probs = jnp.exp(scores - log_total[index][:, :, None])
        seq_values = lax.dynamic_slice_in_dim(values, base, SEQ_LEN, 0)
        grad_block = lax.dynamic_slice_in_dim(grad_mixed, start, block, 0)
        grad_probs = jnp.einsum(
            "qhd,khd->hqk", grad_block, seq_values, preferred_element_type=jnp.float32
        )
        inner = jnp.sum(probs * grad_probs, axis=2, keepdims=True)
        grad_scores = (probs * (grad_probs - inner)).astype(jnp.bfloat16)
        part_query = (
            jnp.einsum("hqk,khd->qhd", grad_scores, window, preferred_element_type=jnp.float32)
            * scale
        )
        part_keys = (
            jnp.einsum("hqk,qhd->khd", grad_scores, picked, preferred_element_type=jnp.float32)
            * scale
        )
        part_values = jnp.einsum(
            "hqk,qhd->khd",
            probs.astype(jnp.bfloat16),
            grad_block,
            preferred_element_type=jnp.float32,
        )
        grad_query = lax.dynamic_update_slice_in_dim(grad_query, part_query, start, 0)
        grad_keys = lax.dynamic_update_slice_in_dim(
            grad_keys, lax.dynamic_slice_in_dim(grad_keys, base, SEQ_LEN, 0) + part_keys, base, 0
        )
        grad_values = lax.dynamic_update_slice_in_dim(
            grad_values,
            lax.dynamic_slice_in_dim(grad_values, base, SEQ_LEN, 0) + part_values,
            base,
            0,
        )
        return (grad_query, grad_keys, grad_values)

    return lax.fori_loop(0, rows // block, one_block, (zeros, zeros, zeros))


def shards(
    hidden_in,
    teacher,
    valid_mask,
    first_gain,
    second_gain,
    attention_in,
    attention_out,
    feed_in,
    feed_out,
):
    columns = lax.axis_size("col")
    own_rows = hidden_in.shape[0]
    group = own_rows * columns
    own_start = lax.axis_index("col") * own_rows
    group_start = lax.axis_index("row") * group
    total_tokens = group * lax.axis_size("row")
    live_group = lax.dynamic_slice_in_dim(valid_mask, group_start, group, 0)
    live_own = lax.dynamic_slice_in_dim(live_group, own_start, own_rows, 0).astype(jnp.float32)
    valid_total = jnp.sum(valid_mask.astype(jnp.float32))
    joint_rows, attention_rows, feed_in_rows, feed_out_rows = (
        lax.all_gather(attention_in, "row", axis=2, tiled=True),
        lax.all_gather(attention_out, "row", axis=0, tiled=True),
        lax.all_gather(feed_in, "row", axis=2, tiled=True),
        lax.all_gather(feed_out, "row", axis=0, tiled=True),
    )
    inputs = hidden_in.astype(jnp.float32)
    normed_one, inverse_one, low_one = layer_norm(inputs, first_gain)
    joint = jnp.einsum(
        "rd,icd->ric",
        lax.all_gather(low_one, "col", axis=0, tiled=True),
        joint_rows,
        preferred_element_type=jnp.float32,
    )
    local_width = joint.shape[2]
    split = (group, local_width // HD, HD)
    cosine, sine = rotary_tables(group, HD)
    query = rotate(joint[:, 0].reshape(split), cosine, sine).astype(jnp.bfloat16)
    keys = rotate(joint[:, 1].reshape(split), cosine, sine).astype(jnp.bfloat16)
    values = joint[:, 2].reshape(split).astype(jnp.bfloat16)
    mixed, log_total = attend(query, keys, values, live_group)
    part = mixed
    branch = lax.psum_scatter(
        jnp.einsum("rc,oc->ro", part, attention_rows, preferred_element_type=jnp.float32),
        "col",
        scatter_dimension=0,
        tiled=True,
    )
    middle = inputs + branch
    normed_two, inverse_two, low_two = layer_norm(middle, second_gain)
    projected = jnp.einsum(
        "rd,ifd->rif",
        lax.all_gather(low_two, "col", axis=0, tiled=True),
        feed_in_rows,
        preferred_element_type=jnp.float32,
    )
    gate = projected[:, 0]
    upper = projected[:, 1]
    activated = (jax.nn.gelu(gate, approximate=False) * upper).astype(jnp.bfloat16)
    part = activated
    feed_branch = lax.psum_scatter(
        jnp.einsum("rf,of->ro", part, feed_out_rows, preferred_element_type=jnp.float32),
        "col",
        scatter_dimension=0,
        tiled=True,
    )
    result = middle + feed_branch
    error_term = result - teacher
    squares = jnp.sum(live_own * jnp.sum(error_term * error_term, axis=1))
    grad_result = (total_tokens * live_own)[:, None] * error_term / valid_total
    grad_low = grad_result.astype(jnp.bfloat16)
    piece = lax.all_gather(grad_low, "col", axis=0, tiled=True)
    part = activated
    grad_out = jnp.einsum("ro,rf->of", piece, part, preferred_element_type=jnp.float32)
    rows_grad = jnp.einsum("ro,of->rf", piece, feed_out_rows, preferred_element_type=jnp.float32)
    grad_act = rows_grad

    def geglu(first, second):
        return jax.nn.gelu(first, approximate=False) * second

    unused, pull = jax.vjp(geglu, gate, upper)
    grad_gate, grad_upper = pull(grad_act)
    grad_projected = jnp.stack([grad_gate, grad_upper], axis=1).astype(jnp.bfloat16)
    part = grad_projected
    grad_low_two = lax.psum_scatter(
        jnp.einsum("rif,ifd->rd", part, feed_in_rows, preferred_element_type=jnp.float32),
        "col",
        scatter_dimension=0,
        tiled=True,
    )
    grad_middle_norm, grad_second = norm_back(grad_low_two, normed_two, inverse_two, second_gain)
    grad_middle = grad_result + grad_middle_norm
    grad_branch = grad_middle.astype(jnp.bfloat16)
    piece = lax.all_gather(grad_branch, "col", axis=0, tiled=True)
    part = mixed
    grad_weight = jnp.einsum("ro,rc->oc", piece, part, preferred_element_type=jnp.float32)
    rows_grad = jnp.einsum("ro,oc->rc", piece, attention_rows, preferred_element_type=jnp.float32)
    grad_heads = rows_grad
    grad_attention_rows, grad_heads = (grad_weight, grad_heads)
    grad_mixed = grad_heads.astype(jnp.bfloat16)
    grad_query, grad_keys, grad_values = attend_back(
        query, keys, values, live_group, log_total, grad_mixed.reshape(split)
    )
    grad_joint = jnp.stack(
        [rotate_back(grad_query, cosine, sine), rotate_back(grad_keys, cosine, sine), grad_values],
        axis=1,
    )
    grad_joint = grad_joint.astype(jnp.bfloat16).reshape(group, 3, local_width)
    part = grad_joint
    grad_low_one = lax.psum_scatter(
        jnp.einsum("ric,icd->rd", part, joint_rows, preferred_element_type=jnp.float32).astype(
            jnp.bfloat16
        ),
        "col",
        scatter_dimension=0,
        tiled=True,
    ).astype(jnp.float32)
    grad_input_norm, grad_first = norm_back(grad_low_one, normed_one, inverse_one, first_gain)
    grad_input = grad_middle + grad_input_norm
    grad_joint_weight = jnp.einsum(
        "ric,rd->icd",
        grad_joint,
        lax.all_gather(low_one, "col", axis=0, tiled=True),
        preferred_element_type=jnp.float32,
    )
    grad_feed_weight = jnp.einsum(
        "rif,rd->ifd",
        grad_projected,
        lax.all_gather(low_two, "col", axis=0, tiled=True),
        preferred_element_type=jnp.float32,
    )
    grads = (
        lax.psum_scatter(
            grad_joint_weight.astype(jnp.bfloat16), "row", scatter_dimension=2, tiled=True
        ).astype(jnp.float32),
        lax.psum_scatter(
            grad_attention_rows.astype(jnp.bfloat16), "row", scatter_dimension=0, tiled=True
        ).astype(jnp.float32),
        lax.psum_scatter(
            grad_feed_weight.astype(jnp.bfloat16), "row", scatter_dimension=2, tiled=True
        ).astype(jnp.float32),
        lax.psum_scatter(
            grad_out.astype(jnp.bfloat16), "row", scatter_dimension=0, tiled=True
        ).astype(jnp.float32),
    )
    totals = lax.psum((grad_first, grad_second, squares), ("row", "col"))
    loss = totals[2] / (D * valid_total)
    return (
        result.astype(jnp.bfloat16),
        loss,
        grad_input,
        totals[0],
        totals[1],
        grads[0],
        grads[1],
        grads[2],
        grads[3],
    )


def solution(mesh):
    in_specs = (
        P(("row", "col"), None),
        P(("row", "col"), None),
        P(),
        P(),
        P(),
        P(None, "col", "row"),
        P("row", "col"),
        P(None, "col", "row"),
        P("row", "col"),
    )
    out_specs = (
        P(("row", "col"), None),
        P(),
        P(("row", "col"), None),
        P(),
        P(),
        P(None, "col", "row"),
        P("row", "col"),
        P(None, "col", "row"),
        P("row", "col"),
    )
    return jax.shard_map(shards, mesh=mesh, in_specs=in_specs, out_specs=out_specs, check_vma=False)
```

profile of v0, /device:TPU:0, one launch (start us, length us, event | category | flops | bytes accessed | tf_op | source)
XLA Modules:
  0.0 1042.4 jit_solution(1975161616662650184)
XLA Ops:
  13.8 36.6 %all_gather.28 = bf16[1024,256]{1,0:T(8,128)(2,1)} all-gather(bf16[128,256]{1,0:T(8,128)(2,1)S(1)} %copy-done.23), channel_id=1, replica_groups=mesh['row'=8,'col'=4] {'row'}, dimensions={0}, use_global_device_ids=true | all-gather | bytes 589824 | tf_op jit(solution)/shard_map/all_gather | solution.py:149
  60.2 35.2 %all-gather.8.cloned.1.call-done = bf16[2048,1024]{1,0:T(8,128)(2,1)} async-done(((bf16[512,1024]{1,0:T(8,128)(2,1)}), bf16[2048,1024]{1,0:T(8,128)(2,1)}) %all-gather.8.cloned.1.call-update) | async-done | bytes 4194320 | tf_op jit(solution)/shard_map/all_gather | solution.py:157
  104.2 52.4 %while.30 = (s32[]{:T(128)}, bf16[4,512,4,64]{1,3,2,0:T(8,128)(2,1)}, f32[4,4,512]{2,1,0:T(4,128)S(1)}, s32[2048]{0:T(1024)S(1)}, s32[4]{0:T(128)S(1)}, /*index=...) while((s32[]{:T(128)}, ...), condition=%wide.region_5.6_spmd, body=%wide.region_2.5_spmd.sunk | while | flops 1124204544 | bytes 53035200 | solution.py:76
  166.1 70.8 %reduce-scatter.15.cloned.1.call-done = f32[512,1024]{1,0:T(8,128)} async-done(((f32[2048,1024]{1,0:T(8,128)}), f32[512,1024]{1,0:T(8,128)}) %reduce-scatter.15.cloned.1.call-update) | async-done | bytes 2097168 | tf_op jit(solution)/shard_map/reduce_scatter | solution.py:169
  241.4 54.6 %all-gather.14.cloned.1.call-done = bf16[2,656,1024]{2,1,0:T(8,128)(2,1)} async-done(((bf16[2,656,128]{2,1,0:T(8,128)(2,1)}), bf16[2,656,1024]{2,1,0:T(8,128)(2,1)}) %all-gather.14.cloned.1.call-update) | async-done | bytes 2686992 | tf_op jit(solution)/shard_map/all_gather | solution.py:150
  296.0 34.6 %all-gather.12.cloned.1.call-done = bf16[2048,1024]{1,0:T(8,128)(2,1)} async-done(((bf16[512,1024]{1,0:T(8,128)(2,1)}), bf16[2048,1024]{1,0:T(8,128)(2,1)}) %all-gather.12.cloned.1.call-update) | async-done | bytes 4194320 | tf_op jit(solution)/shard_map/all_gather | solution.py:179
  343.3 12.9 %multiply_convert_fusion.2 = (bf16[2048,656]{0,1:T(8,128)(2,1)}, f32[2048,656]{0,1:T(8,128)}) fusion(f32[2048,2,656]{0,2,1:T(8,128)S(1)} %fusion.59), kind=kLoop, calls=%fused_computation.63 | loop fusion | flops 88670208 | bytes 18808832 | tf_op jit(solution)/shard_map/convert_element_type | solution.py:185
  356.1 18.4 %all-gather.16.cloned.1.call-done = bf16[1024,656]{0,1:T(8,128)(2,1)} async-done(((bf16[128,656]{0,1:T(8,128)(2,1)}), bf16[1024,656]{0,1:T(8,128)(2,1)}) %all-gather.16.cloned.1.call-update) | async-done | bytes 1343504 | tf_op jit(solution)/shard_map/all_gather | solution.py:151
  374.5 8.9 fusion.111
  384.9 68.3 %reduce-scatter.17.cloned.1.call-done = f32[512,1024]{1,0:T(8,128)} async-done(((f32[2048,1024]{1,0:T(8,128)}), f32[512,1024]{1,0:T(8,128)}) %reduce-scatter.17.cloned.1.call-update) | async-done | bytes 2097168 | tf_op jit(solution)/shard_map/reduce_scatter | solution.py:187
  457.7 34.3 %all-gather.18.cloned.1.call-done = bf16[2048,1024]{1,0:T(8,128)(2,1)} async-done(((bf16[512,1024]{1,0:T(8,128)(2,1)}), bf16[2048,1024]{1,0:T(8,128)(2,1)}) %all-gather.18.cloned.1.call-update) | async-done | bytes 4194320 | tf_op jit(solution)/shard_map/all_gather | solution.py:198
  492.0 10.4 %fusion.66 = (bf16[2048,1,656]{0,2,1:T(8,128)(2,1)S(1)}, bf16[2048,1,656]{0,2,1:T(8,128)(2,1)S(1)}) fusion(f32[2048,656]{0,1:T(8,128)} %get-tuple-element.310, f32[2048,2,656]{0,2,1:T(8,128)} %copy-done.8, bf16[2048,1024]{1,0:T(8,128)(2,1)} %all-gather.18.cloned.1.call-done, bf16[1024,656]{0,1:T(8,128)(2,1)} %all-gather.16.cloned.1.call-done), kind=kOutput, calls=%fused_computation.92 | convolution fusion | flops 2775646208 | bytes 27033600 | tf_op jit(solution)/shard_map/ro,of->rf/dot_general | solution.py:201
  504.9 9.0 convolution_bitcast_fusion
  514.0 71.5 %reduce-scatter.19.cloned.1.call-done = f32[512,1024]{1,0:T(8,128)} async-done(((f32[2048,1024]{1,0:T(8,128)}), f32[512,1024]{1,0:T(8,128)}) %reduce-scatter.19.cloned.1.call-update) | async-done | bytes 2097168 | tf_op jit(solution)/shard_map/reduce_scatter | solution.py:211
  601.2 10.7 %fusion.74 = bf16[2,656,1024]{2,1,0:T(8,128)(2,1)} fusion(bf16[2048,1024]{1,0:T(8,128)(2,1)} %all-gather.12.cloned.1.call-done, bf16[2048,1,656]{0,2,1:T(8,128)(2,1)} %copy-done.33, bf16[2048,1,656]{0,2,1:T(8,128)(2,1)} %copy-done.32), kind=kOutput, calls=%fused_computation.103 | convolution fusion | flops 5506957312 | bytes 12255232 | tf_op jit(solution)/shard_map/rif,rd->ifd/dot_general | solution.py:252
  635.0 167.3 %while.31 = (s32[]{:T(128)}, f32[2048,4,64]{0,2,1:T(8,128)}, f32[2048,4,64]{0,2,1:T(8,128)}, f32[2048,4,64]{0,2,1:T(8,128)}, s32[2048]{0:T(1024)S(1)}, /*index=5...) while((s32[]{:T(128)}, f32[2048,4,64]{0,2,1:T(8,128)}, ...), condition=%wide.region_19.20_spmd.clone, body=%wide.region_17.19_spmd.clone.sunk | while | flops 2750021632 | bytes 172564736 | solution.py:124
  644.1 9.4 multiply_reduce_fusion.8
  685.5 9.4 multiply_reduce_fusion.8
  727.6 9.4 multiply_reduce_fusion.8
  769.8 9.4 multiply_reduce_fusion.8
  851.7 23.2 %reduce-scatter.23.cloned.1.call-done = bf16[128,256]{1,0:T(8,128)(2,1)} async-done(((bf16[1024,256]{1,0:T(8,128)(2,1)}), bf16[128,256]{1,0:T(8,128)(2,1)}) %reduce-scatter.23.cloned.1.call-update) | async-done | bytes 65552 | tf_op jit(solution)/shard_map/reduce_scatter | solution.py:262
  876.4 66.4 %reduce-scatter.25.cloned.1.call-done = bf16[128,768]{1,0:T(8,128)(2,1)} async-done(((bf16[1024,768]{1,0:T(8,128)(2,1)}), bf16[128,768]{1,0:T(8,128)(2,1)}) %reduce-scatter.25.cloned.1.call-update) | async-done | bytes 196624
  946.4 42.2 %reduce-scatter.21.cloned.1.call-done = bf16[512,1024]{1,0:T(8,128)(2,1)} async-done(((bf16[2048,1024]{1,0:T(8,128)(2,1)}), bf16[512,1024]{1,0:T(8,128)(2,1)}) %reduce-scatter.21.cloned.1.call-update) | async-done | bytes 1048592 | tf_op jit(solution)/shard_map/reduce_scatter | solution.py:236
  990.9 39.7 %all-reduce = (f32[]{:T(128)}, f32[1024]{0:T(1024)}, f32[1024]{0:T(1024)}) all-reduce(f32[]{:T(128)} %multiply_reduce_fusion.6, f32[1024]{0:T(1024)S(1)} %get-tuple-element.264, f32[1024]{0:T(1024)S(1)} %copy-done.30), channel_id=1, replica_groups=mesh['row'=8,'col'=4] {'row','col'}, use_global_device_ids=true, to_apply=%region_12.13 | all-reduce | flops 2049 | bytes 16392 | tf_op jit(solution)/shard_map/psum | solution.py:272
  (230 shorter events, 336.7 us)
Async XLA Ops:
  7.2 53.0 %all-gather.10.cloned.1.call-start = ((), (), s32[]{:S(2)}) async-start(), calls=%async_computation.9 | async-start | bytes 1769472 | tf_op jit(solution)/shard_map/all_gather | solution.py:148
  7.9 87.5 %all-gather.8.cloned.1.call-start = ((), (), s32[]{:S(2)}) async-start(), calls=%async_computation.8 | async-start | bytes 5242880 | tf_op jit(solution)/shard_map/all_gather | solution.py:157
  13.7 223.2 %reduce-scatter.15.cloned.1.call-start = ((), (), s32[]{:S(2)}) async-start(), calls=%async_computation.10 | async-start | bytes 10485760 | tf_op jit(solution)/shard_map/reduce_scatter | solution.py:169
  156.6 8.7 copy-start.1
  165.3 74.1 %copy-start.26 = (f32[1024]{0:T(1024)S(1)}, f32[1024]{0:T(1024)}, u32[]{:S(2)}) copy-start(f32[1024]{0:T(1024)} %param.17) | copy-start | bytes 12292
  165.3 130.7 %all-gather.14.cloned.1.call-start = ((), (), s32[]{:S(2)}) async-start(), calls=%async_computation.12 | async-start | bytes 3022848 | tf_op jit(solution)/shard_map/all_gather | solution.py:150
  165.9 164.7 %all-gather.12.cloned.1.call-start = ((), (), s32[]{:S(2)}) async-start(), calls=%async_computation.11 | async-start | bytes 5242880 | tf_op jit(solution)/shard_map/all_gather | solution.py:179
  240.7 133.8 %all-gather.16.cloned.1.call-start = ((), (), s32[]{:S(2)}) async-start(), calls=%async_computation.13 | async-start | bytes 1511424 | tf_op jit(solution)/shard_map/all_gather | solution.py:151
  241.3 211.9 %reduce-scatter.17.cloned.1.call-start = ((), (), s32[]{:S(2)}) async-start(), calls=%async_computation.14 | async-start | bytes 10485760 | tf_op jit(solution)/shard_map/reduce_scatter | solution.py:187
  383.4 108.6 %all-gather.18.cloned.1.call-start = ((), (), s32[]{:S(2)}) async-start(), calls=%async_computation.15 | async-start | bytes 5242880 | tf_op jit(solution)/shard_map/all_gather | solution.py:198
  457.4 128.0 %reduce-scatter.19.cloned.1.call-start = ((), (), s32[]{:S(2)}) async-start(), calls=%async_computation.16 | async-start | bytes 10485760 | tf_op jit(solution)/shard_map/reduce_scatter | solution.py:211
  492.0 12.9 %copy-start.31 = (bf16[2,656,1024]{2,1,0:T(8,128)(2,1)S(1)}, bf16[2,656,1024]{2,1,0:T(8,128)(2,1)}, u32[]{:S(2)}) copy-start(bf16[2,656,1024]{2,1,0:T(8,128)(2,1)} %all-gather.14.cloned.1.call-done) | copy-start | bytes 8060932
  513.9 115.0 %all-gather.20.cloned.1.call-start = ((), (), s32[]{:S(2)}) async-start(), calls=%async_computation.17 | async-start | bytes 5242880 | tf_op jit(solution)/shard_map/all_gather | solution.py:220
  593.6 250.1 %reduce-scatter.29.cloned.1.call-start = ((), (), s32[]{:S(2)}) async-start(), calls=%async_computation.22 | async-start | bytes 1769472
  601.2 244.5 %reduce-scatter.27.cloned.1.call-start = ((), (), s32[]{:S(2)}) async-start(), calls=%async_computation.21 | async-start | bytes 3244032
  628.4 246.6 %reduce-scatter.23.cloned.1.call-start = ((), (), s32[]{:S(2)}) async-start(), calls=%async_computation.19 | async-start | bytes 589824 | tf_op jit(solution)/shard_map/reduce_scatter | solution.py:262
  812.2 130.6 %reduce-scatter.25.cloned.1.call-start = ((), (), s32[]{:S(2)}) async-start(), calls=%async_computation.20 | async-start | bytes 1769472
  835.3 153.3 %reduce-scatter.21.cloned.1.call-start = ((), (), s32[]{:S(2)}) async-start(), calls=%async_computation.18 | async-start | bytes 5242880 | tf_op jit(solution)/shard_map/reduce_scatter | solution.py:236
  842.8 145.8 %copy-start.3 = (bf16[512,1024]{1,0:T(8,128)(2,1)S(1)}, bf16[512,1024]{1,0:T(8,128)(2,1)}, u32[]{:S(2)}) copy-start(bf16[512,1024]{1,0:T(8,128)(2,1)} %param.13) | copy-start | bytes 3145732
  842.8 145.8 %copy-start.25 = (f32[512]{0:T(512)S(1)}, f32[512]{0:T(512)}, u32[]{:S(2)}) copy-start(f32[512]{0:T(512)} %copy-done.24) | copy-start | bytes 6148
  842.8 145.8 %copy-start.27 = (f32[1024]{0:T(1024)S(1)}, f32[1024]{0:T(1024)}, u32[]{:S(2)}) copy-start(f32[1024]{0:T(1024)} %param.16) | copy-start | bytes 12292
  842.8 145.8 %copy-start.29 = (f32[512]{0:T(512)S(1)}, f32[512]{0:T(512)}, u32[]{:S(2)}) copy-start(f32[512]{0:T(512)} %copy-done.28) | copy-start | bytes 6148
  842.9 148.0 %copy-start.30 = (f32[1024]{0:T(1024)S(1)}, f32[1024]{0:T(1024)}, u32[]{:S(2)}) copy-start(f32[1024]{0:T(1024)} %get-tuple-element.261) | copy-start | bytes 12292
  842.9 188.4 %copy-start.10 = (f32[512,1024]{1,0:T(8,128)S(1)}, f32[512,1024]{1,0:T(8,128)}, u32[]{:S(2)}) copy-start(f32[512,1024]{1,0:T(8,128)} %get-tuple-element.308) | copy-start | bytes 6291460
  (29 other events, 106.1 us)
Sparse Core Ops, SparseCore 0:
  10.0 50.0 all-gather.9
  62.3 33.0 all-gather.7
  165.4 71.4 reduce-scatter.14
  238.8 57.1 all-gather.13
  298.0 32.6 all-gather.11
  332.5 41.9 all-gather.15
  383.6 69.5 reduce-scatter.16
  457.6 34.4 all-gather.17
  514.0 71.3 reduce-scatter.18
  593.7 34.4 all-gather.19
  631.6 65.7 reduce-scatter.28
  700.9 71.3 reduce-scatter.26
  812.4 62.5 reduce-scatter.22
  878.2 64.6 reduce-scatter.24
  945.2 43.3 reduce-scatter.20
where the time goes:
time: 1050 us; the launch traced here: 1040 us
  waiting for transfers between devices  529 us (50%)
  matrix products  241 us (23%)
  other arithmetic  112 us (11%)
  blocking collectives  76.3 us (7%)
  local copies, waits for them, and re-layouts  62.1 us (6%)
  between operations  17.3 us (2%)
    reduce_scatter x1, waiting for transfers between devices, shards(): lax.psum_scatter(jnp.einsum('rif,ifd->rd', part, feed_in_rows, preferred_...  71.5 us
    reduce_scatter x1, waiting for transfers between devices, shards(): lax.psum_scatter(jnp.einsum('rc,oc->ro', part, attention_rows, preferred_...  70.8 us
    unnamed x18, waiting for transfers between devices  68.4 us
    reduce_scatter x1, waiting for transfers between devices, shards(): lax.psum_scatter(jnp.einsum('rf,of->ro', part, feed_out_rows, preferred_e...  68.3 us
    all_gather x1, waiting for transfers between devices, shards(): lax.all_gather(feed_in, 'row', axis=2, tiled=True)  54.6 us
    reduce_scatter x1, waiting for transfers between devices, shards(): lax.psum_scatter(jnp.einsum('ric,icd->rd', part, joint_rows, preferred_el...  42.2 us
    psum x1, blocking collectives, shards(): totals = lax.psum((grad_first, grad_second, squares), ('row', 'col'))  39.7 us
    unnamed x77, local copies, waits for them, and re-layouts  38.5 us
  transfers between devices with their start and end apart: 15, of which 12 were waited for; matrix products, arithmetic and copies ran while one was open for 27% of the time, Pallas kernels for 0%

commit v1 on v0

--- a/solution.py
+++ b/solution.py
@@ -9,6 +9,28 @@
 EPSILON = 1e-05
 ROPE_BASE = 160000.0
 FLOOR_SCORE = -1e30
+
+
+def in_order(blocks, dim):
+    shape = list(blocks.shape[1:])
+    shape[dim] *= blocks.shape[0]
+    return jnp.moveaxis(blocks, 0, dim).reshape(shape)
+
+
+def gather_around(array, axis, dim):
+    length = lax.axis_size(axis)
+    pairs = [(i, (i + 1) % length) for i in range(length)]
+    back = [(b, a) for a, b in pairs]
+    lower, upper = ([], [])
+    for turn in range(length - 1):
+        if turn % 2 == 0:
+            lower.append(lax.ppermute(lower[-1] if lower else array, axis, pairs))
+        else:
+            upper.append(lax.ppermute(upper[-1] if upper else array, axis, back))
+    blocks = jnp.stack([*lower[::-1], array, *upper])
+    shift = lax.axis_index(axis) - len(lower)
+    blocks = blocks[(jnp.arange(length) - shift) % length]
+    return in_order(blocks, dim)
 
 
 def layer_norm(values, gain):
@@ -147,7 +169,7 @@
     joint_rows, attention_rows, feed_in_rows, feed_out_rows = (
         lax.all_gather(attention_in, "row", axis=2, tiled=True),
         lax.all_gather(attention_out, "row", axis=0, tiled=True),
-        lax.all_gather(feed_in, "row", axis=2, tiled=True),
+        gather_around(feed_in, "row", 2),
         lax.all_gather(feed_out, "row", axis=0, tiled=True),
     )
     inputs = hidden_in.astype(jnp.float32)

time: 1050 us -> 1020 us (0.971)
  waiting for transfers between devices: 529 us -> 451 us
  starting transfers between devices: 1.47 us -> 31.1 us
  local copies, waits for them, and re-layouts: 62.1 us -> 78.9 us
    all_gather x1 -> x0, waiting for transfers between devices: 54.6 us -> none  [shards(): lax.all_gather(feed_in, 'row', axis=2, tiled=True)]
    all_gather x1, waiting for transfers between devices: 34.6 us -> 0.01 us  [shards(): lax.all_gather(low_two, 'col', axis=0, tiled=True)]
    ppermute x0 -> x7, starting transfers between devices: none -> 29.6 us  [the longest x3 23.1 us: gather_around(): upper.append(lax.ppermute(upper[-1] if upper else array, axis, back))]
    ppermute x0 -> x7, waiting for transfers between devices: none -> 29 us  [the longest x4 29 us: gather_around(): lower.append(lax.ppermute(lower[-1] if lower else array, axis, pairs))]
    all_gather x1, waiting for transfers between devices: 18.4 us -> 0.01 us  [shards(): lax.all_gather(feed_out, 'row', axis=0, tiled=True)]
    unnamed x77 -> x92, local copies, waits for them, and re-layouts: 38.5 us -> 50.3 us
    unnamed x18 -> x17, waiting for transfers between devices: 68.4 us -> 67.4 us
  transfers between devices with their start and end apart: 15 -> 21, of which waited for: 12 -> 13; matrix products, arithmetic and copies ran while one was open for 27% -> 29% of each run, Pallas kernels for 0% -> 0%
where the time goes in v1:
time: 1020 us; the launch traced here: 1010 us
  waiting for transfers between devices  451 us (44%)
  matrix products  241 us (24%)
  other arithmetic  112 us (11%)
  local copies, waits for them, and re-layouts  78.9 us (8%)
  blocking collectives  76.3 us (7%)
  starting transfers between devices  31.1 us (3%)
  between operations  17.3 us (2%)
    reduce_scatter x1, waiting for transfers between devices, shards(): lax.psum_scatter(jnp.einsum('rif,ifd->rd', part, feed_in_rows, preferred_...  71.5 us
    reduce_scatter x1, waiting for transfers between devices, shards(): lax.psum_scatter(jnp.einsum('rc,oc->ro', part, attention_rows, preferred_...  71.3 us
    reduce_scatter x1, waiting for transfers between devices, shards(): lax.psum_scatter(jnp.einsum('rf,of->ro', part, feed_out_rows, preferred_e...  69.1 us
    unnamed x17, waiting for transfers between devices  67.4 us
    unnamed x92, local copies, waits for them, and re-layouts  50.3 us
    reduce_scatter x1, waiting for transfers between devices, shards(): lax.psum_scatter(jnp.einsum('ric,icd->rd', part, joint_rows, preferred_el...  42.2 us
    psum x1, blocking collectives, shards(): totals = lax.psum((grad_first, grad_second, squares), ('row', 'col'))  39.7 us
    dot_general x4, matrix products, one_block(): jnp.einsum('qhd,khd->hqk', grad_block, seq_values, preferred_element_type...  37.7 us
  transfers between devices with their start and end apart: 21, of which 13 were waited for; matrix products, arithmetic and copies ran while one was open for 29% of the time, Pallas kernels for 0%

profile of v1, /device:TPU:0, one launch (start us, length us, event | category | flops | bytes accessed | tf_op | source)
XLA Modules:
  0.0 1010.6 jit_solution(4973920490419649821)
XLA Ops:
  13.8 36.7 %all_gather.25 = bf16[1024,256]{1,0:T(8,128)(2,1)} all-gather(bf16[128,256]{1,0:T(8,128)(2,1)S(1)} %copy-done.28), channel_id=1, replica_groups=mesh['row'=8,'col'=4] {'row'}, dimensions={0}, use_global_device_ids=true | all-gather | bytes 589824 | tf_op jit(solution)/shard_map/all_gather | solution.py:171
  60.2 35.2 %all-gather.7.cloned.1.call-done = bf16[2048,1024]{1,0:T(8,128)(2,1)} async-done(((bf16[512,1024]{1,0:T(8,128)(2,1)}), bf16[2048,1024]{1,0:T(8,128)(2,1)}) %all-gather.7.cloned.1.call-update) | async-done | bytes 4194320 | tf_op jit(solution)/shard_map/all_gather | solution.py:179
  104.2 52.4 %while.30 = (s32[]{:T(128)}, bf16[4,512,4,64]{1,3,2,0:T(8,128)(2,1)}, f32[4,4,512]{2,1,0:T(4,128)S(1)}, s32[2048]{0:T(1024)S(1)}, s32[4]{0:T(128)S(1)}, /*index=...) while((s32[]{:T(128)}, ...), condition=%wide.region_5.6_spmd, body=%wide.region_2.0_spmd.sunk | while | flops 1124204544 | bytes 53035200 | solution.py:98
  165.6 71.3 %reduce-scatter.15.cloned.1.call-done = f32[512,1024]{1,0:T(8,128)} async-done(((f32[2048,1024]{1,0:T(8,128)}), f32[512,1024]{1,0:T(8,128)}) %reduce-scatter.15.cloned.1.call-update) | async-done | bytes 2097168 | tf_op jit(solution)/shard_map/reduce_scatter | solution.py:191
  242.4 10.7 %collective-permute-done = bf16[2,656,128]{2,1,0:T(8,128)(2,1)S(1)} collective-permute-done((bf16[2,656,128]{2,1,0:T(8,128)(2,1)S(1)}, bf16[2,656,128]{2,1,0:T(8,128)(2,1)S(1)}, u32[]{:S(2)}, u32[]{:S(2)}) %collective-permute-start) | collective-permute-done | bytes 335904 | tf_op jit(solution)/shard_map/ppermute | solution.py:27
  257.8 8.9 collective-permute-done.1
  284.9 10.0 collective-permute-start.6
  328.3 12.9 %multiply_convert_fusion.2 = (bf16[2048,656]{0,1:T(8,128)(2,1)}, f32[2048,656]{0,1:T(8,128)}) fusion(f32[2048,2,656]{0,2,1:T(8,128)S(1)} %fusion.59), kind=kLoop, calls=%fused_computation.64 | loop fusion | flops 88670208 | bytes 18808832 | tf_op jit(solution)/shard_map/convert_element_type | solution.py:207
  341.2 9.0 fusion.117
  351.7 69.1 %reduce-scatter.17.cloned.1.call-done = f32[512,1024]{1,0:T(8,128)} async-done(((f32[2048,1024]{1,0:T(8,128)}), f32[512,1024]{1,0:T(8,128)}) %reduce-scatter.17.cloned.1.call-update) | async-done | bytes 2097168 | tf_op jit(solution)/shard_map/reduce_scatter | solution.py:209
  425.3 34.3 %all-gather.15.cloned.1.call-done = bf16[2048,1024]{1,0:T(8,128)(2,1)} async-done(((bf16[512,1024]{1,0:T(8,128)(2,1)}), bf16[2048,1024]{1,0:T(8,128)(2,1)}) %all-gather.15.cloned.1.call-update) | async-done | bytes 4194320 | tf_op jit(solution)/shard_map/all_gather | solution.py:220
  459.6 10.4 %fusion.68 = (bf16[2048,1,656]{0,2,1:T(8,128)(2,1)S(1)}, bf16[2048,1,656]{0,2,1:T(8,128)(2,1)S(1)}) fusion(f32[2048,656]{0,1:T(8,128)} %get-tuple-element.310, f32[2048,2,656]{0,2,1:T(8,128)} %copy-done.9, bf16[2048,1024]{1,0:T(8,128)(2,1)} %all-gather.15.cloned.1.call-done, bf16[1024,656]{0,1:T(8,128)(2,1)} %all-gather.13.cloned.1.call-done), kind=kOutput, calls=%fused_computation.95 | convolution fusion | flops 2775646208 | bytes 27033600 | tf_op jit(solution)/shard_map/ro,of->rf/dot_general | solution.py:223
  472.4 9.0 convolution_bitcast_fusion
  481.5 71.5 %reduce-scatter.19.cloned.1.call-done = f32[512,1024]{1,0:T(8,128)} async-done(((f32[2048,1024]{1,0:T(8,128)}), f32[512,1024]{1,0:T(8,128)}) %reduce-scatter.19.cloned.1.call-update) | async-done | bytes 2097168 | tf_op jit(solution)/shard_map/reduce_scatter | solution.py:233
  568.8 10.8 %fusion.78 = bf16[2,656,1024]{2,1,0:T(8,128)(2,1)} fusion(bf16[2048,1024]{1,0:T(8,128)(2,1)} %all-gather.11.cloned.1.call-done, bf16[2048,1,656]{0,2,1:T(8,128)(2,1)} %copy-done.37, bf16[2048,1,656]{0,2,1:T(8,128)(2,1)} %copy-done.36), kind=kOutput, calls=%fused_computation.108 | convolution fusion | flops 5506957312 | bytes 12255232 | tf_op jit(solution)/shard_map/rif,rd->ifd/dot_general | solution.py:274
  602.8 167.4 %while.31 = (s32[]{:T(128)}, f32[2048,4,64]{0,2,1:T(8,128)}, f32[2048,4,64]{0,2,1:T(8,128)}, f32[2048,4,64]{0,2,1:T(8,128)}, s32[2048]{0:T(1024)S(1)}, /*index=5...) while((s32[]{:T(128)}, f32[2048,4,64]{0,2,1:T(8,128)}, ...), condition=%wide.region_19.20_spmd.clone, body=%wide.region_17.19_spmd.clone.sunk | while | flops 2750021632 | bytes 172564736 | solution.py:146
  612.0 9.5 multiply_reduce_fusion.8
  653.4 9.4 multiply_reduce_fusion.8
  695.4 9.5 multiply_reduce_fusion.8
  737.7 9.4 multiply_reduce_fusion.8
  819.4 23.7 %reduce-scatter.23.cloned.1.call-done = bf16[128,256]{1,0:T(8,128)(2,1)} async-done(((bf16[1024,256]{1,0:T(8,128)(2,1)}), bf16[128,256]{1,0:T(8,128)(2,1)}) %reduce-scatter.23.cloned.1.call-update) | async-done | bytes 65552 | tf_op jit(solution)/shard_map/reduce_scatter | solution.py:284
  844.6 66.5 %reduce-scatter.25.cloned.1.call-done = bf16[128,768]{1,0:T(8,128)(2,1)} async-done(((bf16[1024,768]{1,0:T(8,128)(2,1)}), bf16[128,768]{1,0:T(8,128)(2,1)}) %reduce-scatter.25.cloned.1.call-update) | async-done | bytes 196624
  914.6 42.2 %reduce-scatter.21.cloned.1.call-done = bf16[512,1024]{1,0:T(8,128)(2,1)} async-done(((bf16[2048,1024]{1,0:T(8,128)(2,1)}), bf16[512,1024]{1,0:T(8,128)(2,1)}) %reduce-scatter.21.cloned.1.call-update) | async-done | bytes 1048592 | tf_op jit(solution)/shard_map/reduce_scatter | solution.py:258
  959.1 39.7 %all-reduce = (f32[]{:T(128)}, f32[1024]{0:T(1024)}, f32[1024]{0:T(1024)}) all-reduce(f32[]{:T(128)} %multiply_reduce_fusion.6, f32[1024]{0:T(1024)S(1)} %get-tuple-element.264, f32[1024]{0:T(1024)S(1)} %copy-done.35), channel_id=1, replica_groups=mesh['row'=8,'col'=4] {'row','col'}, use_global_device_ids=true, to_apply=%region_12.13 | all-reduce | flops 2049 | bytes 16392 | tf_op jit(solution)/shard_map/psum | solution.py:294
  (260 shorter events, 380.8 us)
Async XLA Ops:
  7.2 53.0 %all-gather.9.cloned.1.call-start = ((), (), s32[]{:S(2)}) async-start(), calls=%async_computation.9 | async-start | bytes 1769472 | tf_op jit(solution)/shard_map/all_gather | solution.py:170
  7.9 87.5 %all-gather.7.cloned.1.call-start = ((), (), s32[]{:S(2)}) async-start(), calls=%async_computation.8 | async-start | bytes 5242880 | tf_op jit(solution)/shard_map/all_gather | solution.py:179
  13.7 223.2 %reduce-scatter.15.cloned.1.call-start = ((), (), s32[]{:S(2)}) async-start(), calls=%async_computation.10 | async-start | bytes 10485760 | tf_op jit(solution)/shard_map/reduce_scatter | solution.py:191
  165.4 150.3 %all-gather.11.cloned.1.call-start = ((), (), s32[]{:S(2)}) async-start(), calls=%async_computation.11 | async-start | bytes 5242880 | tf_op jit(solution)/shard_map/all_gather | solution.py:201
  240.8 100.4 %all-gather.13.cloned.1.call-start = ((), (), s32[]{:S(2)}) async-start(), calls=%async_computation.12 | async-start | bytes 1511424 | tf_op jit(solution)/shard_map/all_gather | solution.py:173
  240.9 12.2 %collective-permute-start = (bf16[2,656,128]{2,1,0:T(8,128)(2,1)S(1)}, bf16[2,656,128]{2,1,0:T(8,128)(2,1)S(1)}, u32[]{:S(2)}, u32[]{:S(2)}) collective-permute-start(bf16[2,656,128]{2,1,0:T(8,128)(2,1)S(1)} %copy-done.25), channel_id=1, source_target_pairs={{0,4},{4,8},{8,12},{12,16},{16,20},{20,24},{24,28},{28,0},{1,5},{5... | collective-permute-start | bytes 1007624 | tf_op jit(solution)/shard_map/ppermute | solution.py:27
  253.0 13.6 %collective-permute-start.1 = (bf16[2,656,128]{2,1,0:T(8,128)(2,1)S(1)}, bf16[2,656,128]{2,1,0:T(8,128)(2,1)S(1)}, u32[]{:S(2)}, u32[]{:S(2)}) collective-permute-start(bf16[2,656,128]{2,1,0:T(8,128)(2,1)S(1)} %collective-permute-done), channel_id=1, source_target_pairs={{0,4},{4,8},{8,12},{12,16},{16,20},{20,24},{24,28},{28,0},{1,5},{5... | collective-permute-start | bytes 1007624 | tf_op jit(solution)/shard_map/ppermute | solution.py:27
  253.0 16.1 %collective-permute-start.4 = (bf16[2,656,128]{2,1,0:T(8,128)(2,1)S(1)}, bf16[2,656,128]{2,1,0:T(8,128)(2,1)}, u32[]{:S(2)}, u32[]{:S(2)}) collective-permute-start(bf16[2,656,128]{2,1,0:T(8,128)(2,1)S(1)} %copy-done.25), channel_id=1, source_target_pairs={{4,0},{8,4},{12,8},{16,12},{20,16},{24,20},{28,24},{0,28},{5,1},{9... | collective-permute-start | bytes 1007624 | tf_op jit(solution)/shard_map/ppermute | solution.py:29
  266.6 15.6 %collective-permute-start.2 = (bf16[2,656,128]{2,1,0:T(8,128)(2,1)S(1)}, bf16[2,656,128]{2,1,0:T(8,128)(2,1)}, u32[]{:S(2)}, u32[]{:S(2)}) collective-permute-start(bf16[2,656,128]{2,1,0:T(8,128)(2,1)S(1)} %collective-permute-done.1), channel_id=1, source_target_pairs={{0,4},{4,8},{8,12},{12,16},{16,20},{20,24},{24,28},{28,0},{1,5},{5... | collective-permute-start | bytes 1007624 | tf_op jit(solution)/shard_map/ppermute | solution.py:27
  269.1 15.8 %collective-permute-start.5 = (bf16[2,656,128]{2,1,0:T(8,128)(2,1)}, bf16[2,656,128]{2,1,0:T(8,128)(2,1)}, u32[]{:S(2)}, u32[]{:S(2)}) collective-permute-start(bf16[2,656,128]{2,1,0:T(8,128)(2,1)} %collective-permute-done.4), channel_id=1, source_target_pairs={{4,0},{8,4},{12,8},{16,12},{20,16},{24,20},{28,24},{0,28},{5,1},{9... | collective-permute-start | bytes 1007624 | tf_op jit(solution)/shard_map/ppermute | solution.py:29
  282.2 17.4 %collective-permute-start.3 = (bf16[2,656,128]{2,1,0:T(8,128)(2,1)}, bf16[2,656,128]{2,1,0:T(8,128)(2,1)}, u32[]{:S(2)}, u32[]{:S(2)}) collective-permute-start(bf16[2,656,128]{2,1,0:T(8,128)(2,1)} %collective-permute-done.2), channel_id=1, source_target_pairs={{0,4},{4,8},{8,12},{12,16},{16,20},{20,24},{24,28},{28,0},{1,5},{5... | collective-permute-start | bytes 1007624 | tf_op jit(solution)/shard_map/ppermute | solution.py:27
  284.8 136.0 %reduce-scatter.17.cloned.1.call-start = ((), (), s32[]{:S(2)}) async-start(), calls=%async_computation.13 | async-start | bytes 10485760 | tf_op jit(solution)/shard_map/reduce_scatter | solution.py:209
  284.9 25.9 %collective-permute-start.6 = (bf16[2,656,128]{2,1,0:T(8,128)(2,1)}, bf16[2,656,128]{2,1,0:T(8,128)(2,1)S(1)}, u32[]{:S(2)}, u32[]{:S(2)}) collective-permute-start(bf16[2,656,128]{2,1,0:T(8,128)(2,1)} %collective-permute-done.5), channel_id=1, source_target_pairs={{4,0},{8,4},{12,8},{16,12},{20,16},{24,20},{28,24},{0,28},{5,1},{9... | collective-permute-start | bytes 1007624 | tf_op jit(solution)/shard_map/ppermute | solution.py:29
  350.2 109.5 %all-gather.15.cloned.1.call-start = ((), (), s32[]{:S(2)}) async-start(), calls=%async_computation.14 | async-start | bytes 5242880 | tf_op jit(solution)/shard_map/all_gather | solution.py:220
  425.0 128.0 %reduce-scatter.19.cloned.1.call-start = ((), (), s32[]{:S(2)}) async-start(), calls=%async_computation.15 | async-start | bytes 10485760 | tf_op jit(solution)/shard_map/reduce_scatter | solution.py:233
  481.5 114.8 %all-gather.17.cloned.1.call-start = ((), (), s32[]{:S(2)}) async-start(), calls=%async_computation.16 | async-start | bytes 5242880 | tf_op jit(solution)/shard_map/all_gather | solution.py:242
  561.1 250.4 %reduce-scatter.29.cloned.1.call-start = ((), (), s32[]{:S(2)}) async-start(), calls=%async_computation.21 | async-start | bytes 1769472
  568.7 244.6 %reduce-scatter.27.cloned.1.call-start = ((), (), s32[]{:S(2)}) async-start(), calls=%async_computation.20 | async-start | bytes 3244032
  595.8 247.3 %reduce-scatter.23.cloned.1.call-start = ((), (), s32[]{:S(2)}) async-start(), calls=%async_computation.18 | async-start | bytes 589824 | tf_op jit(solution)/shard_map/reduce_scatter | solution.py:284
  780.2 130.9 %reduce-scatter.25.cloned.1.call-start = ((), (), s32[]{:S(2)}) async-start(), calls=%async_computation.19 | async-start | bytes 1769472
  803.2 153.7 %reduce-scatter.21.cloned.1.call-start = ((), (), s32[]{:S(2)}) async-start(), calls=%async_computation.17 | async-start | bytes 5242880 | tf_op jit(solution)/shard_map/reduce_scatter | solution.py:258
  810.7 146.2 %copy-start.4 = (bf16[512,1024]{1,0:T(8,128)(2,1)S(1)}, bf16[512,1024]{1,0:T(8,128)(2,1)}, u32[]{:S(2)}) copy-start(bf16[512,1024]{1,0:T(8,128)(2,1)} %param.13) | copy-start | bytes 3145732
  810.7 146.1 %copy-start.30 = (f32[512]{0:T(512)S(1)}, f32[512]{0:T(512)}, u32[]{:S(2)}) copy-start(f32[512]{0:T(512)} %copy-done.29) | copy-start | bytes 6148
  814.8 184.6 %copy-start.11 = (f32[512,1024]{1,0:T(8,128)S(1)}, f32[512,1024]{1,0:T(8,128)}, u32[]{:S(2)}) copy-start(f32[512,1024]{1,0:T(8,128)} %get-tuple-element.308) | copy-start | bytes 6291460
  (39 other events, 655.9 us)
Sparse Core Ops, SparseCore 0:
  10.0 50.0 all-gather.8
  62.3 33.0 all-gather.6
  165.5 71.4 reduce-scatter.14
  240.9 34.4 all-gather.10
  284.9 43.1 all-gather.12
  350.3 70.4 reduce-scatter.16
  425.2 34.4 all-gather.14
  481.6 71.4 reduce-scatter.18
  561.2 34.4 all-gather.16
  599.0 65.7 reduce-scatter.28
  668.4 71.0 reduce-scatter.26
  780.3 62.7 reduce-scatter.22
  846.5 64.5 reduce-scatter.24
  913.5 43.3 reduce-scatter.20
